TPU v7x, 32 devices: a whole 2x2x4 slice. The times are simulated.
32 devices in a mesh: dp: 2 (over core), expert: 16 (over z, y, x).
Axes of the slice: x: 2, y: 2, z: 4, core: 2. Of those that a mesh axis runs over, the one named last changes fastest.
Arguments:
- tokens: bfloat16 [2048, 2048], P('expert'), may hold values from -6 to 6
- out_grad: bfloat16 [2048, 2048], P('expert'), may hold values from -6 to 6
- route_ids: int32 [2048, 8], P('expert'), may hold values from 0 to 15, all different within a row; in each aligned block of 128 rows (0 to 127, 128 to 255, ...) at most 72 rows name the same one
- route_probs: float32 [2048, 8], P('expert'), may hold values from 0.05 to 1
- gate_store: bfloat16 [16, 2048, 768], P(None, 'expert', 'dp'), may hold values from -0.125 to 0.125
- up_store: bfloat16 [16, 2048, 768], P(None, 'expert', 'dp'), may hold values from -0.125 to 0.125
- down_store: bfloat16 [16, 2048, 768], P(None, 'expert', 'dp'), may hold values from -0.21875 to 0.21875
Outputs:
- grad_gate: bfloat16 [16, 2048, 768], P('expert', None, 'dp')
- grad_up: bfloat16 [16, 2048, 768], P('expert', None, 'dp')
- grad_down: bfloat16 [16, 2048, 768], P('expert', None, 'dp')
- grad_tokens: bfloat16 [2048, 2048], P('expert')
Inputs may be any that keep to these rules, and one draw needn't show every extreme that they name: `route_ids`: among the 128 tokens of one device no expert is named more than 72 times, and in every draw some expert is named exactly 72 times by some device's tokens.
All inputs are finite; a program needn't handle non-finite values.
Results may differ from a plain program's by a relative error of at most 0.0065.
Values may be sent and summed in bfloat16 or wider, within the bound.
A program may use at most 128 MiB of HBM per device.

v0:
```python
import jax
import jax.numpy as jnp
from jax import lax
from jax.sharding import PartitionSpec as P


def on_device(tokens, out_grad, route_ids, route_probs, gate_store, up_store, down_store):
    tok_rows, model_width = tokens.shape
    top_count = route_ids.shape[1]
    experts = lax.axis_size("expert")
    capacity = max(2, 9 * tok_rows * top_count // (8 * experts))
    slot_total = tok_rows * top_count
    flat_ids = route_ids.reshape(-1)
    expert_range = jnp.arange(experts, dtype=jnp.int32)
    per_count = jnp.sum((flat_ids[:, None] == expert_range[None, :]).astype(jnp.int32), axis=0)
    offsets = jnp.cumsum(per_count) - per_count
    order = jnp.argsort(flat_ids, stable=True)
    sorted_ids = flat_ids[order]
    sorted_rank = jnp.arange(slot_total, dtype=jnp.int32) - offsets[sorted_ids]
    slot_rank = jnp.zeros((slot_total,), jnp.int32).at[order].set(sorted_rank)
    slot_place = flat_ids * capacity + slot_rank
    source = (
        jnp.full((experts * capacity,), slot_total, jnp.int32)
        .at[slot_place]
        .set(jnp.arange(slot_total, dtype=jnp.int32))
    )
    filled = source < slot_total
    safe_index = jnp.where(filled, source, 0)
    owner_row = safe_index // top_count
    x_slots = jnp.where(filled[:, None], tokens[owner_row], jnp.zeros((), jnp.bfloat16))
    slot_prob = jnp.where(filled, route_probs.reshape(-1)[safe_index], 0.0)
    dy_slots = (slot_prob[:, None] * out_grad[owner_row].astype(jnp.float32)).astype(jnp.bfloat16)
    x_slots = x_slots.reshape(experts, capacity, model_width)
    dy_slots = dy_slots.reshape(experts, capacity, model_width)
    gate_all, up_all, down_all = (
        lax.all_to_all(gate_store, "expert", split_axis=0, concat_axis=1, tiled=True),
        lax.all_to_all(up_store, "expert", split_axis=0, concat_axis=1, tiled=True),
        lax.all_to_all(down_store, "expert", split_axis=0, concat_axis=1, tiled=True),
    )
    gate_panel = gate_all[0]
    up_panel = up_all[0]
    col_width = model_width // lax.axis_size("dp")
    col_start = lax.axis_index("dp") * col_width
    x_part = lax.dynamic_slice_in_dim(x_slots, col_start, col_width, 2)
    dy_part = lax.dynamic_slice_in_dim(dy_slots, col_start, col_width, 2)
    x_sent, dy_sent = (
        lax.all_to_all(x_part, "expert", split_axis=0, concat_axis=0, tiled=True),
        lax.all_to_all(dy_part, "expert", split_axis=0, concat_axis=0, tiled=True),
    )
    x_in, dy_in = (
        lax.all_gather(x_sent, "dp", axis=2, tiled=True),
        lax.all_gather(dy_sent, "dp", axis=2, tiled=True),
    )
    rows_in = x_in.reshape(-1, model_width)
    dy_rows = dy_in.reshape(-1, model_width)
    gate_pre = jnp.dot(rows_in, gate_panel, preferred_element_type=jnp.float32)
    up_pre = jnp.dot(rows_in, up_panel, preferred_element_type=jnp.float32)
    sigmoid_gate = jax.nn.sigmoid(gate_pre)
    activation = (gate_pre * sigmoid_gate * up_pre).astype(jnp.bfloat16)
    down_panel = down_all[0]
    act_grad = jnp.dot(dy_rows, down_panel, preferred_element_type=jnp.float32)
    up_grad = (act_grad * gate_pre * sigmoid_gate).astype(jnp.bfloat16)
    gate_grad = (act_grad * up_pre * sigmoid_gate * (1.0 + gate_pre * (1.0 - sigmoid_gate))).astype(
        jnp.bfloat16
    )
    contract = (((0,), (0,)), ((), ()))
    grad_down = lax.dot_general(
        dy_rows, activation, contract, preferred_element_type=jnp.float32
    ).astype(jnp.bfloat16)
    grad_gate = lax.dot_general(
        rows_in, gate_grad, contract, preferred_element_type=jnp.float32
    ).astype(jnp.bfloat16)
    grad_up = lax.dot_general(
        rows_in, up_grad, contract, preferred_element_type=jnp.float32
    ).astype(jnp.bfloat16)
    back_contract = (((1,), (1,)), ((), ()))
    slot_half = lax.dot_general(
        gate_grad, gate_panel, back_contract, preferred_element_type=jnp.float32
    ) + lax.dot_general(up_grad, up_panel, back_contract, preferred_element_type=jnp.float32)
    summed = lax.psum_scatter(
        slot_half.reshape(experts, capacity, model_width), "dp", scatter_dimension=2, tiled=True
    )
    returned = lax.all_to_all(
        summed.astype(jnp.bfloat16), "expert", split_axis=0, concat_axis=0, tiled=True
    )
    share_width = returned.shape[2]
    slot_values = returned.reshape(experts * capacity, share_width)[slot_place]
    token_share = jnp.sum(
        slot_values.reshape(tok_rows, top_count, share_width).astype(jnp.float32), axis=1
    ).astype(jnp.bfloat16)
    grad_tokens = lax.all_gather(token_share, "dp", axis=1, tiled=True)
    return (grad_gate[None], grad_up[None], grad_down[None], grad_tokens)


def gathered(tokens, out_grad, route_ids, route_probs, gate_store, up_store, down_store):
    tok_rows, model_width = tokens.shape
    experts = lax.axis_size("expert")
    half = tok_rows // lax.axis_size("dp")
    start = lax.axis_index("dp") * half
    both = ("expert", "dp")
    chosen = route_ids[:, :, None] == jnp.arange(experts, dtype=jnp.int32)[None, None, :]
    weight = jnp.sum(jnp.where(chosen, route_probs[:, :, None], 0.0), axis=1)
    weight = lax.all_to_all(
        weight.T.reshape(experts, tok_rows), "expert", split_axis=0, concat_axis=0, tiled=True
    )
    weight = weight.reshape(-1, 1)
    x_all = lax.all_gather(
        lax.dynamic_slice_in_dim(tokens, start, half, 0), both, axis=0, tiled=True
    )
    g_all = lax.all_gather(
        lax.dynamic_slice_in_dim(out_grad, start, half, 0), both, axis=0, tiled=True
    )
    gate_panel, up_panel, down_panel = (
        lax.all_to_all(store, "expert", split_axis=0, concat_axis=1, tiled=True)[0]
        for store in (gate_store, up_store, down_store)
    )
    gate_pre = jnp.dot(x_all, gate_panel, preferred_element_type=jnp.float32)
    up_pre = jnp.dot(x_all, up_panel, preferred_element_type=jnp.float32)
    act_grad = jnp.dot(g_all, down_panel, preferred_element_type=jnp.float32) * weight
    sig = jax.nn.sigmoid(gate_pre)
    activation = (gate_pre * sig * up_pre * weight).astype(jnp.bfloat16)
    up_grad = (act_grad * gate_pre * sig).astype(jnp.bfloat16)
    gate_grad = (act_grad * up_pre * sig * (1.0 + gate_pre * (1.0 - sig))).astype(jnp.bfloat16)
    back = (((1,), (1,)), ((), ()))
    slot_half = lax.dot_general(
        gate_grad, gate_panel, back, preferred_element_type=jnp.float32
    ) + lax.dot_general(up_grad, up_panel, back, preferred_element_type=jnp.float32)
    share = lax.psum_scatter(slot_half.astype(jnp.bfloat16), both, scatter_dimension=0, tiled=True)
    grad_tokens = lax.all_gather(share, "dp", axis=0, tiled=True)
    outer = (((0,), (0,)), ((), ()))
    grad_down = lax.dot_general(
        g_all, activation, outer, preferred_element_type=jnp.float32
    ).astype(jnp.bfloat16)
    grad_gate = lax.dot_general(x_all, gate_grad, outer, preferred_element_type=jnp.float32).astype(
        jnp.bfloat16
    )
    grad_up = lax.dot_general(x_all, up_grad, outer, preferred_element_type=jnp.float32).astype(
        jnp.bfloat16
    )
    return (grad_gate[None], grad_up[None], grad_down[None], grad_tokens)


def choose(tokens, out_grad, route_ids, *rest):
    if lax.axis_size("expert") <= 2 * route_ids.shape[1]:
        return gathered(tokens, out_grad, route_ids, *rest)
    return on_device(tokens, out_grad, route_ids, *rest)


def solution(mesh):
    return jax.shard_map(
        choose,
        mesh=mesh,
        in_specs=(
            P("expert", None),
            P("expert", None),
            P("expert", None),
            P("expert", None),
            P(None, "expert", "dp"),
            P(None, "expert", "dp"),
            P(None, "expert", "dp"),
        ),
        out_specs=(
            P("expert", None, "dp"),
            P("expert", None, "dp"),
            P("expert", None, "dp"),
            P("expert", None),
        ),
        check_vma=False,
    )
```

profile of v0, /device:TPU:0, one launch (start us, length us, event | category | flops | bytes accessed | tf_op | source)
XLA Modules:
  0.0 414.2 jit_solution(4239823326702032732)
XLA Ops:
  7.2 1.0 copy-done
  8.2 0.7 constant_dynamic-slice_fusion.1
  9.0 0.0 all-gather.5.cloned.1.call-start
  9.0 1.7 constant_dynamic-slice_fusion
  10.7 0.8 select_reduce_fusion
  11.6 15.4 %all_to_all.36 = f32[16,1,128]{2,1,0:T(1,128)S(1)} all-to-all(f32[16,1,128]{2,1,0:T(1,128)S(1)} %bitcast.34), channel_id=1, replica_groups=mesh['dp'=2,'expert'=16] {'expert'}, dimensions={0} | all-to-all | bytes 16384 | tf_op jit(solution)/shard_map/all_to_all | solution.py:103
  27.0 52.7 %all_to_all.37 = bf16[16,128,384]{2,1,0:T(8,128)(2,1)} all-to-all(bf16[16,128,384]{2,1,0:T(8,128)(2,1)} %param.11), channel_id=1, replica_groups=mesh['dp'=2,'expert'=16] {'expert'}, dimensions={0} | all-to-all | bytes 3145728 | tf_op jit(solution)/shard_map/all_to_all | solution.py:114
  79.7 56.4 %all_to_all.38 = bf16[16,128,384]{2,1,0:T(8,128)(2,1)S(1)} all-to-all(bf16[16,128,384]{2,1,0:T(8,128)(2,1)S(1)} %copy-done.7), channel_id=1, replica_groups=mesh['dp'=2,'expert'=16] {'expert'}, dimensions={0} | all-to-all | bytes 3145728 | tf_op jit(solution)/shard_map/all_to_all | solution.py:114
  136.1 4.6 %all-to-all-start = ((bf16[16,128,384]{2,1,0:T(8,128)(2,1)}), bf16[16,128,384]{2,1,0:T(8,128)(2,1)}, u32[]{:S(2)}, u32[]{:S(2)}) async-start(bf16[16,128,384]{2,1,0:T(8,128)(2,1)} %param.13), calls=%async_computation | async-start | bytes 3145728 | tf_op jit(solution)/shard_map/all_to_all | solution.py:114
  140.7 0.0 reduce-scatter.2.cloned.1.call-start
  140.8 10.2 %fusion.7 = f32[2048,384]{1,0:T(8,128)} fusion(bf16[2048,2048]{1,0:T(8,128)(2,1)} %all-gather.3.cloned.1.call-done, bf16[2048,384]{1,0:T(8,128)(2,1)} %bitcast.32), kind=kOutput, calls=%fused_computation.20 | convolution fusion | flops 3221225472 | bytes 13107200 | tf_op jit(solution)/shard_map/dot_general | solution.py:117
  151.0 6.4 %fusion.6 = f32[2048,384]{1,0:T(8,128)} fusion(bf16[2048,2048]{1,0:T(8,128)(2,1)S(1)} %copy-done.8, bf16[2048,384]{1,0:T(8,128)(2,1)S(1)} %bitcast.30), kind=kOutput, calls=%fused_computation.19 | convolution fusion | flops 3221225472 | bytes 13107200 | tf_op jit(solution)/shard_map/dot_general | solution.py:118
  157.3 30.6 %all-to-all-done = bf16[16,128,384]{2,1,0:T(8,128)(2,1)} async-done(((bf16[16,128,384]{2,1,0:T(8,128)(2,1)}), bf16[16,128,384]{2,1,0:T(8,128)(2,1)}, u32[]{:S(2)}, u32[]{:S(2)}) %all-to-all-start) | async-done | bytes 1572896 | tf_op jit(solution)/shard_map/all_to_all | solution.py:114
  187.9 37.2 %all-gather.5.cloned.1.call-done = bf16[2048,2048]{1,0:T(8,128)(2,1)} async-done(((bf16[64,2048]{1,0:T(8,128)(2,1)}), bf16[2048,2048]{1,0:T(8,128)(2,1)}) %all-gather.5.cloned.1.call-update) | async-done | bytes 8388624 | tf_op jit(solution)/shard_map/all_gather | solution.py:110
  225.1 11.5 %multiply_convert_fusion.1 = (bf16[2048,384]{1,0:T(8,128)(2,1)S(1)}, bf16[2048,384]{1,0:T(8,128)(2,1)S(1)}) fusion(f32[2048,384]{1,0:T(8,128)} %fusion.7, f32[2048,384]{1,0:T(8,128)} %fusion.6, f32[2048]{0:T(1024)S(1)} %bitcast.35, bf16[2048,2048]{1,0:T(8,128)(2,1)} %all-gather.5.cloned.1.call-done, bf16[2048,384]{1,0:T(8,128)(2,1)} %bitcast), kind=kOutput, calls=%fused_computation.2 | convolution fusion | flops 3232235520 | bytes 19406848 | tf_op jit(solution)/shard_map/dot_general | solution.py:119
  236.7 8.2 %fusion.8 = f32[2048,2048]{1,0:T(8,128)} fusion(bf16[2048,384]{1,0:T(8,128)(2,1)S(1)} %get-tuple-element.5, bf16[2048,384]{1,0:T(8,128)(2,1)S(1)} %bitcast.33), kind=kOutput, calls=%fused_computation.21 | convolution fusion | flops 3221225472 | bytes 19922944 | tf_op jit(solution)/shard_map/dot_general | solution.py:125
  244.9 10.3 %add_convert_fusion = bf16[2048,2048]{1,0:T(8,128)(2,1)} fusion(f32[2048,2048]{1,0:T(8,128)} %fusion.8, bf16[2048,384]{1,0:T(8,128)(2,1)S(1)} %get-tuple-element.4, bf16[2048,384]{1,0:T(8,128)(2,1)S(1)} %bitcast.31), kind=kOutput, calls=%fused_computation | convolution fusion | flops 3229614080 | bytes 28311552 | tf_op jit(solution)/shard_map/dot_general | solution.py:127
  255.2 1.4 copy-done.6
  256.6 9.3 %fusion.1 = bf16[1,2048,384]{2,1,0:T(8,128)(2,1)} fusion(bf16[2048,2048]{1,0:T(8,128)(2,1)} %all-gather.3.cloned.1.call-done, bf16[2048,384]{1,0:T(8,128)(2,1)S(1)} %copy-done.6), kind=kOutput, calls=%fused_computation.10 | convolution fusion | flops 3222011904 | bytes 11534336 | tf_op jit(solution)/shard_map/dot_general | solution.py:137
  266.0 9.4 %fusion = bf16[1,2048,384]{2,1,0:T(8,128)(2,1)} fusion(bf16[2048,2048]{1,0:T(8,128)(2,1)} %all-gather.3.cloned.1.call-done, bf16[2048,384]{1,0:T(8,128)(2,1)S(1)} %copy-done.4), kind=kOutput, calls=%fused_computation.9 | convolution fusion | flops 3222011904 | bytes 11534336 | tf_op jit(solution)/shard_map/dot_general | solution.py:134
  275.4 6.0 %fusion.2 = bf16[1,2048,384]{2,1,0:T(8,128)(2,1)} fusion(bf16[2048,2048]{1,0:T(8,128)(2,1)S(1)} %bitcast.38, f32[2048,384]{1,0:T(8,128)S(1)} %copy-done.10, f32[2048,384]{1,0:T(8,128)S(1)} %copy-done.9, f32[2048]{0:T(1024)S(1)} %bitcast.36), kind=kOutput, calls=%fused_computation.11 | convolution fusion | flops 3227516928 | bytes 16261120 | tf_op jit(solution)/shard_map/dot_general | solution.py:131
  281.4 123.1 %reduce-scatter.2.cloned.1.call-done = bf16[64,2048]{1,0:T(8,128)(2,1)} async-done(((bf16[2048,2048]{1,0:T(8,128)(2,1)}), bf16[64,2048]{1,0:T(8,128)(2,1)}) %reduce-scatter.2.cloned.1.call-update) | async-done | bytes 262160 | tf_op jit(solution)/shard_map/reduce_scatter | solution.py:128
  404.5 2.4 all_gather.11
  406.8 0.8 copy.19
  (30 shorter events, 0.2 us)
Async XLA Ops:
  7.2 1.1 copy-start
  7.2 133.6 %all-gather.3.cloned.1.call-start = ((), (), s32[]{:S(2)}) async-start(), calls=%async_computation.5 | async-start | bytes 8650752 | tf_op jit(solution)/shard_map/all_gather | solution.py:107
  9.0 216.2 %all-gather.5.cloned.1.call-start = ((), (), s32[]{:S(2)}) async-start(), calls=%async_computation.6 | async-start | bytes 8650752 | tf_op jit(solution)/shard_map/all_gather | solution.py:110
  10.7 69.0 %copy-start.7 = (bf16[16,128,384]{2,1,0:T(8,128)(2,1)S(1)}, bf16[16,128,384]{2,1,0:T(8,128)(2,1)}, u32[]{:S(2)}) copy-start(bf16[16,128,384]{2,1,0:T(8,128)(2,1)} %param.12) | copy-start | bytes 4718596
  136.1 51.8 %all-to-all-start = ((bf16[16,128,384]{2,1,0:T(8,128)(2,1)}), bf16[16,128,384]{2,1,0:T(8,128)(2,1)}, u32[]{:S(2)}, u32[]{:S(2)}) async-start(bf16[16,128,384]{2,1,0:T(8,128)(2,1)} %param.13), calls=%async_computation | async-start | bytes 3145728 | tf_op jit(solution)/shard_map/all_to_all | solution.py:114
  140.7 263.7 %reduce-scatter.2.cloned.1.call-start = ((), (), s32[]{:S(2)}) async-start(), calls=%async_computation.7 | async-start | bytes 8650752 | tf_op jit(solution)/shard_map/reduce_scatter | solution.py:128
  140.8 10.2 %copy-start.8 = (bf16[2048,2048]{1,0:T(8,128)(2,1)S(1)}, bf16[2048,2048]{1,0:T(8,128)(2,1)}, u32[]{:S(2)}) copy-start(bf16[2048,2048]{1,0:T(8,128)(2,1)} %all-gather.3.cloned.1.call-done) | copy-start | bytes 25165828
  225.1 11.6 %copy-start.2 = (bf16[16,128,384]{2,1,0:T(8,128)(2,1)S(1)}, bf16[16,128,384]{2,1,0:T(8,128)(2,1)}, u32[]{:S(2)}) copy-start(bf16[16,128,384]{2,1,0:T(8,128)(2,1)} %all_to_all.37) | copy-start | bytes 4718596
  236.7 8.2 %copy-start.3 = (bf16[2048,384]{1,0:T(8,128)(2,1)}, bf16[2048,384]{1,0:T(8,128)(2,1)S(1)}, u32[]{:S(2)}) copy-start(bf16[2048,384]{1,0:T(8,128)(2,1)S(1)} %get-tuple-element.5) | copy-start | bytes 4718596
  236.7 8.2 %copy-start.5 = (bf16[2048,384]{1,0:T(8,128)(2,1)}, bf16[2048,384]{1,0:T(8,128)(2,1)S(1)}, u32[]{:S(2)}) copy-start(bf16[2048,384]{1,0:T(8,128)(2,1)S(1)} %get-tuple-element.4) | copy-start | bytes 4718596
  255.2 1.4 copy-start.6
  256.6 9.3 %copy-start.4 = (bf16[2048,384]{1,0:T(8,128)(2,1)S(1)}, bf16[2048,384]{1,0:T(8,128)(2,1)}, u32[]{:S(2)}) copy-start(bf16[2048,384]{1,0:T(8,128)(2,1)} %copy-done.3) | copy-start | bytes 4718596
  256.6 18.7 %slice-start = ((s8[8388608]{0:T(1024)(128)(4,1)}), s8[4194304]{0:T(1024)(128)(4,1)S(1)}, s32[]{:S(2)}) async-start(s8[8388608]{0:T(1024)(128)(4,1)} %bitcast.37), calls=%async_computation.8 | async-start | bytes 8388608
  266.0 9.4 %slice-start.1 = ((s8[8388608]{0:T(1024)(128)(4,1)}), s8[4194304]{0:T(1024)(128)(4,1)S(1)}, s32[]{:S(2)}) async-start(s8[8388608]{0:T(1024)(128)(4,1)} %bitcast.37), calls=%async_computation.9 | async-start | bytes 8388608
  266.0 9.4 %copy-start.9 = (f32[2048,384]{1,0:T(8,128)S(1)}, f32[2048,384]{1,0:T(8,128)}, u32[]{:S(2)}) copy-start(f32[2048,384]{1,0:T(8,128)} %fusion.7) | copy-start | bytes 9437188
  266.0 9.4 %copy-start.10 = (f32[2048,384]{1,0:T(8,128)S(1)}, f32[2048,384]{1,0:T(8,128)}, u32[]{:S(2)}) copy-start(f32[2048,384]{1,0:T(8,128)} %fusion.6) | copy-start | bytes 9437188
  275.4 132.3 %copy-start.1 = (bf16[128,2048]{1,0:T(8,128)(2,1)S(1)}, bf16[128,2048]{1,0:T(8,128)(2,1)}, u32[]{:S(2)}) copy-start(bf16[128,2048]{1,0:T(8,128)(2,1)} %param.7) | copy-start | bytes 1572868
Sparse Core Ops, SparseCore 0:
  11.4 115.0 all-gather.2
  130.0 95.1 all-gather.4
  255.4 149.0 reduce-scatter.1
where the time goes:
time: 415 us; the launch traced here: 414 us
  waiting for transfers between devices  191 us (46%)
  blocking collectives  127 us (31%)
  matrix products  71.2 us (17%)
  between operations  13.9 us (3%)
  local copies, waits for them, and re-layouts  5.61 us (1%)
  starting transfers between devices  4.7 us (1%)
    reduce_scatter x1, waiting for transfers between devices, gathered(): lax.psum_scatter(slot_half.astype(jnp.bfloat16), both, scatter_dimension=...  123 us
    all_to_all x2, blocking collectives, gathered(): lax.all_to_all(store, 'expert', split_axis=0, concat_axis=1, tiled=True)[0]  109 us
    all_gather x1, waiting for transfers between devices, gathered(): lax.all_gather(lax.dynamic_slice_in_dim(out_grad, start, half, 0), both,...  37.2 us
    all_to_all x1, waiting for transfers between devices, gathered(): lax.all_to_all(store, 'expert', split_axis=0, concat_axis=1, tiled=True)[0]  30.6 us
    all_to_all x1, blocking collectives, gathered(): lax.all_to_all(weight.T.reshape(experts, tok_rows), 'expert', split_axis=...  15.4 us
    dot_general x1, matrix products, gathered(): jnp.dot(g_all, down_panel, preferred_element_type=jnp.float32) * weight  11.5 us
    dot_general x1, matrix products, gathered(): lax.dot_general(up_grad, up_panel, back, preferred_element_type=jnp.float32)  10.3 us
    dot_general x1, matrix products, gathered(): gate_pre = jnp.dot(x_all, gate_panel, preferred_element_type=jnp.float32)  10.2 us
  transfers between devices with their start and end apart: 4, of which 3 were waited for; matrix products, arithmetic and copies ran while one was open for 11% of the time, Pallas kernels for 0%

commit v1 on v0

--- a/solution.py
+++ b/solution.py
@@ -2,6 +2,7 @@
 import jax.numpy as jnp
 from jax import lax
 from jax.sharding import PartitionSpec as P
+from jax.lax import all_to_all, axis_size
 
 
 def on_device(tokens, out_grad, route_ids, route_probs, gate_store, up_store, down_store):
@@ -107,8 +108,9 @@
     x_all = lax.all_gather(
         lax.dynamic_slice_in_dim(tokens, start, half, 0), both, axis=0, tiled=True
     )
-    g_all = lax.all_gather(
-        lax.dynamic_slice_in_dim(out_grad, start, half, 0), both, axis=0, tiled=True
+    page = lax.dynamic_slice_in_dim(out_grad, start, half, 0)
+    g_all = jnp.concatenate(
+        all_to_all(jnp.stack(axis_size(both) * [page], axis=0), both, 0, 0), axis=0
     )
     gate_panel, up_panel, down_panel = (
         lax.all_to_all(store, "expert", split_axis=0, concat_axis=1, tiled=True)[0]

time: 415 us -> 558 us (1.34)
  waiting for transfers between devices: 191 us -> 348 us
  blocking collectives: 127 us -> 99.1 us
  starting transfers between devices: 4.7 us -> 14.1 us
    all_to_all x0 -> x1, waiting for transfers between devices: none -> 107 us  [gathered(): all_to_all(jnp.stack(axis_size(both) * [page], axis=0), both, 0, 0)]
    all_gather x1, waiting for transfers between devices: 0.02 us -> 83.7 us  [gathered(): lax.all_gather(lax.dynamic_slice_in_dim(tokens, start, half, 0), both, ax...]
    all_gather x1 -> x0, waiting for transfers between devices: 37.2 us -> none  [gathered(): lax.all_gather(lax.dynamic_slice_in_dim(out_grad, start, half, 0), both,...]
    all_to_all x2, blocking collectives: 109 us -> 81.2 us  [gathered(): lax.all_to_all(store, 'expert', split_axis=0, concat_axis=1, tiled=True)[0]]
    all_to_all x0 -> x1, starting transfers between devices: none -> 9.63 us  [gathered(): all_to_all(jnp.stack(axis_size(both) * [page], axis=0), both, 0, 0)]
    all_to_all x1, waiting for transfers between devices: 30.6 us -> 37.6 us  [gathered(): lax.all_to_all(store, 'expert', split_axis=0, concat_axis=1, tiled=True)[0]]
  transfers between devices with their start and end apart: 4 -> 4, of which waited for: 3 -> 4; matrix products, arithmetic and copies ran while one was open for 11% -> 9% of each run, Pallas kernels for 0% -> 0%
where the time goes in v1:
time: 558 us; the launch traced here: 557 us
  waiting for transfers between devices  348 us (62%)
  blocking collectives  99.1 us (18%)
  matrix products  75.3 us (13%)
  between operations  14.2 us (3%)
  starting transfers between devices  14.1 us (3%)
  local copies, waits for them, and re-layouts  5.9 us (1%)
    reduce_scatter x1, waiting for transfers between devices, gathered(): lax.psum_scatter(slot_half.astype(jnp.bfloat16), both, scatter_dimension=...  119 us
    all_to_all x1, waiting for transfers between devices, gathered(): all_to_all(jnp.stack(axis_size(both) * [page], axis=0), both, 0, 0)  107 us
    all_gather x1, waiting for transfers between devices, gathered(): lax.all_gather(lax.dynamic_slice_in_dim(tokens, start, half, 0), both, ax...  83.7 us
    all_to_all x2, blocking collectives, gathered(): lax.all_to_all(store, 'expert', split_axis=0, concat_axis=1, tiled=True)[0]  81.2 us
    all_to_all x1, waiting for transfers between devices, gathered(): lax.all_to_all(store, 'expert', split_axis=0, concat_axis=1, tiled=True)[0]  37.6 us
    all_to_all x1, blocking collectives, gathered(): lax.all_to_all(weight.T.reshape(experts, tok_rows), 'expert', split_axis=...  15.4 us
    dot_general x1, matrix products, gathered(): jnp.dot(g_all, down_panel, preferred_element_type=jnp.float32) * weight  11.5 us
  transfers between devices with their start and end apart: 4, of which 4 were waited for; matrix products, arithmetic and copies ran while one was open for 9% of the time, Pallas kernels for 0%

profile of v1, /device:TPU:0, one launch (start us, length us, event | category | flops | bytes accessed | tf_op | source)
XLA Modules:
  0.0 557.4 jit_solution(6860681386524480749)
XLA Ops:
  7.2 0.9 select_reduce_fusion
  8.1 15.4 %all_to_all.41 = f32[16,1,128]{2,1,0:T(1,128)S(1)} all-to-all(f32[16,1,128]{2,1,0:T(1,128)S(1)} %bitcast.35), channel_id=1, replica_groups=mesh['dp'=2,'expert'=16] {'expert'}, dimensions={0} | all-to-all | bytes 16384 | tf_op jit(solution)/shard_map/all_to_all | solution.py:104
  23.5 40.9 %all_to_all.42 = bf16[16,128,384]{2,1,0:T(8,128)(2,1)} all-to-all(bf16[16,128,384]{2,1,0:T(8,128)(2,1)} %param.11), channel_id=1, replica_groups=mesh['dp'=2,'expert'=16] {'expert'}, dimensions={0} | all-to-all | bytes 3145728 | tf_op jit(solution)/shard_map/all_to_all | solution.py:116
  64.4 40.4 %all_to_all.43 = bf16[16,128,384]{2,1,0:T(8,128)(2,1)S(1)} all-to-all(bf16[16,128,384]{2,1,0:T(8,128)(2,1)S(1)} %copy-done.6), channel_id=1, replica_groups=mesh['dp'=2,'expert'=16] {'expert'}, dimensions={0} | all-to-all | bytes 3145728 | tf_op jit(solution)/shard_map/all_to_all | solution.py:116
  104.7 4.4 all-to-all-start.1
  109.2 0.0 all-gather.2.cloned.1.call-start
  109.2 0.7 constant_dynamic-slice_fusion.1
  110.0 37.6 %all-to-all-done.1 = bf16[16,128,384]{2,1,0:T(8,128)(2,1)} async-done(((bf16[16,128,384]{2,1,0:T(8,128)(2,1)}), bf16[16,128,384]{2,1,0:T(8,128)(2,1)}, u32[]{:S(2)}, u32[]{:S(2)}) %all-to-all-start.1) | async-done | bytes 1572896 | tf_op jit(solution)/shard_map/all_to_all | solution.py:116
  147.6 4.3 stack.2
  151.9 9.6 %all-to-all-start = ((bf16[32,64,2048]{2,1,0:T(8,128)(2,1)}), bf16[32,64,2048]{2,1,0:T(8,128)(2,1)}, u32[]{:S(2)}, u32[]{:S(2)}) async-start(bf16[32,64,2048]{2,1,0:T(8,128)(2,1)} %stack.2), calls=%async_computation | async-start | bytes 16777216 | tf_op jit(solution)/shard_map/all_to_all | solution.py:113
  161.5 0.0 reduce-scatter.2.cloned.1.call-start
  161.6 83.7 %all-gather.2.cloned.1.call-done = bf16[2048,2048]{1,0:T(8,128)(2,1)} async-done(((bf16[64,2048]{1,0:T(8,128)(2,1)}), bf16[2048,2048]{1,0:T(8,128)(2,1)}) %all-gather.2.cloned.1.call-update) | async-done | bytes 8388624 | tf_op jit(solution)/shard_map/all_gather | solution.py:108
  245.3 10.1 %fusion.7 = f32[2048,384]{1,0:T(8,128)} fusion(bf16[2048,2048]{1,0:T(8,128)(2,1)} %all-gather.2.cloned.1.call-done, bf16[2048,384]{1,0:T(8,128)(2,1)} %bitcast.33), kind=kOutput, calls=%fused_computation.20 | convolution fusion | flops 3221225472 | bytes 13107200 | tf_op jit(solution)/shard_map/dot_general | solution.py:119
  255.5 6.4 %fusion.6 = f32[2048,384]{1,0:T(8,128)} fusion(bf16[2048,2048]{1,0:T(8,128)(2,1)S(1)} %copy-done.8, bf16[2048,384]{1,0:T(8,128)(2,1)S(1)} %bitcast.31), kind=kOutput, calls=%fused_computation.19 | convolution fusion | flops 3221225472 | bytes 13107200 | tf_op jit(solution)/shard_map/dot_general | solution.py:120
  261.8 107.5 %all-to-all-done = bf16[32,64,2048]{2,1,0:T(8,128)(2,1)} async-done(((bf16[32,64,2048]{2,1,0:T(8,128)(2,1)}), bf16[32,64,2048]{2,1,0:T(8,128)(2,1)}, u32[]{:S(2)}, u32[]{:S(2)}) %all-to-all-start) | async-done | bytes 8388640 | tf_op jit(solution)/shard_map/all_to_all | solution.py:113
  369.3 11.5 %multiply_convert_fusion.1 = (bf16[2048,384]{1,0:T(8,128)(2,1)S(1)}, bf16[2048,384]{1,0:T(8,128)(2,1)S(1)}) fusion(f32[2048,384]{1,0:T(8,128)} %fusion.7, f32[2048,384]{1,0:T(8,128)} %fusion.6, f32[2048]{0:T(1024)S(1)} %bitcast.36, bf16[2048,2048]{1,0:T(8,128)(2,1)} %bitcast, bf16[2048,384]{1,0:T(8,128)(2,1)} %bitcast.1), kind=kOutput, calls=%fused_computation.2 | convolution fusion | flops 3232235520 | bytes 19406848 | tf_op jit(solution)/shard_map/dot_general | solution.py:121
  380.9 8.3 %fusion.8 = f32[2048,2048]{1,0:T(8,128)} fusion(bf16[2048,384]{1,0:T(8,128)(2,1)S(1)} %get-tuple-element.5, bf16[2048,384]{1,0:T(8,128)(2,1)S(1)} %bitcast.34), kind=kOutput, calls=%fused_computation.21 | convolution fusion | flops 3221225472 | bytes 19922944 | tf_op jit(solution)/shard_map/dot_general | solution.py:127
  389.2 10.3 %add_convert_fusion = bf16[2048,2048]{1,0:T(8,128)(2,1)} fusion(f32[2048,2048]{1,0:T(8,128)} %fusion.8, bf16[2048,384]{1,0:T(8,128)(2,1)S(1)} %get-tuple-element.4, bf16[2048,384]{1,0:T(8,128)(2,1)S(1)} %bitcast.32), kind=kOutput, calls=%fused_computation | convolution fusion | flops 3229614080 | bytes 28311552 | tf_op jit(solution)/shard_map/dot_general | solution.py:129
  399.5 9.6 %fusion = bf16[1,2048,384]{2,1,0:T(8,128)(2,1)} fusion(bf16[2048,2048]{1,0:T(8,128)(2,1)} %all-gather.2.cloned.1.call-done, bf16[2048,384]{1,0:T(8,128)(2,1)} %copy-done.5), kind=kOutput, calls=%fused_computation.9 | convolution fusion | flops 3222011904 | bytes 11534336 | tf_op jit(solution)/shard_map/dot_general | solution.py:136
  409.2 9.3 %fusion.1 = bf16[1,2048,384]{2,1,0:T(8,128)(2,1)} fusion(bf16[2048,2048]{1,0:T(8,128)(2,1)} %all-gather.2.cloned.1.call-done, bf16[2048,384]{1,0:T(8,128)(2,1)S(1)} %copy-done.4), kind=kOutput, calls=%fused_computation.10 | convolution fusion | flops 3222011904 | bytes 11534336 | tf_op jit(solution)/shard_map/dot_general | solution.py:139
  418.5 9.6 %fusion.2 = bf16[1,2048,384]{2,1,0:T(8,128)(2,1)} fusion(bf16[2048,2048]{1,0:T(8,128)(2,1)} %bitcast, f32[2048,384]{1,0:T(8,128)S(1)} %copy-done.10, f32[2048,384]{1,0:T(8,128)S(1)} %copy-done.9, f32[2048]{0:T(1024)S(1)} %bitcast.37), kind=kOutput, calls=%fused_computation.11 | convolution fusion | flops 3227516928 | bytes 16261120 | tf_op jit(solution)/shard_map/dot_general | solution.py:133
  428.2 119.3 %reduce-scatter.2.cloned.1.call-done = bf16[64,2048]{1,0:T(8,128)(2,1)} async-done(((bf16[2048,2048]{1,0:T(8,128)(2,1)}), bf16[64,2048]{1,0:T(8,128)(2,1)}) %reduce-scatter.2.cloned.1.call-update) | async-done | bytes 262160 | tf_op jit(solution)/shard_map/reduce_scatter | solution.py:130
  547.4 2.4 all_gather.7
  549.8 0.8 copy.19
  (25 shorter events, 0.1 us)
Async XLA Ops:
  7.2 102.1 %copy-start = (bf16[128,2048]{1,0:T(8,128)(2,1)S(1)}, bf16[128,2048]{1,0:T(8,128)(2,1)}, u32[]{:S(2)}) copy-start(bf16[128,2048]{1,0:T(8,128)(2,1)} %param.7) | copy-start | bytes 1572868
  7.2 57.2 %copy-start.6 = (bf16[16,128,384]{2,1,0:T(8,128)(2,1)S(1)}, bf16[16,128,384]{2,1,0:T(8,128)(2,1)}, u32[]{:S(2)}) copy-start(bf16[16,128,384]{2,1,0:T(8,128)(2,1)} %param.12) | copy-start | bytes 4718596
  64.4 45.6 %copy-start.7 = (bf16[128,2048]{1,0:T(8,128)(2,1)S(1)}, bf16[128,2048]{1,0:T(8,128)(2,1)}, u32[]{:S(2)}) copy-start(bf16[128,2048]{1,0:T(8,128)(2,1)} %param.8) | copy-start | bytes 1572868
  104.7 42.9 %all-to-all-start.1 = ((bf16[16,128,384]{2,1,0:T(8,128)(2,1)}), bf16[16,128,384]{2,1,0:T(8,128)(2,1)}, u32[]{:S(2)}, u32[]{:S(2)}) async-start(bf16[16,128,384]{2,1,0:T(8,128)(2,1)} %param.13), calls=%async_computation.1 | async-start | bytes 3145728 | tf_op jit(solution)/shard_map/all_to_all | solution.py:116
  109.2 136.2 %all-gather.2.cloned.1.call-start = ((), (), s32[]{:S(2)}) async-start(), calls=%async_computation.6 | async-start | bytes 8650752 | tf_op jit(solution)/shard_map/all_gather | solution.py:108
  151.9 217.4 %all-to-all-start = ((bf16[32,64,2048]{2,1,0:T(8,128)(2,1)}), bf16[32,64,2048]{2,1,0:T(8,128)(2,1)}, u32[]{:S(2)}, u32[]{:S(2)}) async-start(bf16[32,64,2048]{2,1,0:T(8,128)(2,1)} %stack.2), calls=%async_computation | async-start | bytes 16777216 | tf_op jit(solution)/shard_map/all_to_all | solution.py:113
  161.5 385.9 %reduce-scatter.2.cloned.1.call-start = ((), (), s32[]{:S(2)}) async-start(), calls=%async_computation.7 | async-start | bytes 8650752 | tf_op jit(solution)/shard_map/reduce_scatter | solution.py:130
  245.3 10.1 %copy-start.8 = (bf16[2048,2048]{1,0:T(8,128)(2,1)S(1)}, bf16[2048,2048]{1,0:T(8,128)(2,1)}, u32[]{:S(2)}) copy-start(bf16[2048,2048]{1,0:T(8,128)(2,1)} %all-gather.2.cloned.1.call-done) | copy-start | bytes 25165828
  369.3 11.6 %copy-start.2 = (bf16[16,128,384]{2,1,0:T(8,128)(2,1)S(1)}, bf16[16,128,384]{2,1,0:T(8,128)(2,1)}, u32[]{:S(2)}) copy-start(bf16[16,128,384]{2,1,0:T(8,128)(2,1)} %all_to_all.42) | copy-start | bytes 4718596
  380.9 8.3 %copy-start.5 = (bf16[2048,384]{1,0:T(8,128)(2,1)}, bf16[2048,384]{1,0:T(8,128)(2,1)S(1)}, u32[]{:S(2)}) copy-start(bf16[2048,384]{1,0:T(8,128)(2,1)S(1)} %get-tuple-element.5) | copy-start | bytes 4718596
  380.9 8.3 %copy-start.3 = (bf16[2048,384]{1,0:T(8,128)(2,1)}, bf16[2048,384]{1,0:T(8,128)(2,1)S(1)}, u32[]{:S(2)}) copy-start(bf16[2048,384]{1,0:T(8,128)(2,1)S(1)} %get-tuple-element.4) | copy-start | bytes 4718596
  399.5 9.7 %copy-start.4 = (bf16[2048,384]{1,0:T(8,128)(2,1)S(1)}, bf16[2048,384]{1,0:T(8,128)(2,1)}, u32[]{:S(2)}) copy-start(bf16[2048,384]{1,0:T(8,128)(2,1)} %copy-done.3) | copy-start | bytes 4718596
  409.2 9.3 %copy-start.9 = (f32[2048,384]{1,0:T(8,128)S(1)}, f32[2048,384]{1,0:T(8,128)}, u32[]{:S(2)}) copy-start(f32[2048,384]{1,0:T(8,128)} %fusion.7) | copy-start | bytes 9437188
  409.2 9.3 %copy-start.10 = (f32[2048,384]{1,0:T(8,128)S(1)}, f32[2048,384]{1,0:T(8,128)}, u32[]{:S(2)}) copy-start(f32[2048,384]{1,0:T(8,128)} %fusion.6) | copy-start | bytes 9437188
  418.5 132.1 %copy-start.1 = (bf16[128,2048]{1,0:T(8,128)(2,1)S(1)}, bf16[128,2048]{1,0:T(8,128)(2,1)}, u32[]{:S(2)}) copy-start(bf16[128,2048]{1,0:T(8,128)(2,1)} %param.7) | copy-start | bytes 1572868
Sparse Core Ops, SparseCore 0:
  113.4 131.8 all-gather.1
  399.6 147.7 reduce-scatter.1
